TPU v7x, 32 devices: a whole 2x2x4 slice. The times are simulated.
32 devices in a mesh: dp: 4 (over y, core), expert: 8 (over z, x).
Axes of the slice: x: 2, y: 2, z: 4, core: 2. Of those that a mesh axis runs over, the one named last changes fastest.
Arguments:
- out_grad: bfloat16 [16384, 3584], P(('dp', 'expert')), may hold values from -6 to 6
- expert_ids: int32 [16384, 8], P(('dp', 'expert')), may hold values from 0 to 255, as said below
- affinity_logits: float32 [16384, 8], P(('dp', 'expert')), may hold values from -6 to 6
- activations: bfloat16 [4, 8, 256, 1024], P('dp', 'expert'), may hold values from -0.29882812 to 0.29882812
- down_weight: bfloat16 [8, 1024, 3584], P('expert', 'dp'), may hold values from -0.1875 to 0.1875
Outputs:
- hidden_grad: bfloat16 [4, 8, 256, 1024], P('dp', 'expert')
- weight_grad: float32 [8, 1024, 3584], P('expert', 'dp')
- logit_grad: float32 [16384, 8], P(('dp', 'expert'))
Inputs may be any that keep to these rules, and one draw needn't show every extreme that they name: `expert_ids`: the k-th id of every token (k counted from 0) is congruent to k modulo 8. In every aligned block of 512 rows no id of the first column is named more than 32 times, and some multiple of 32 is named exactly 32 times.
All inputs are finite; a program needn't handle non-finite values.
Results may differ from a plain program's by a relative error of at most 0.012.
Values may be sent and summed in bfloat16 or wider, within the bound.
A program may use at most 128 MiB of HBM per device.

v0:
```python
import jax
import jax.numpy as jnp
from jax import lax
from jax.sharding import PartitionSpec as P

EXPERTS = 256
TOP = 8


def contract_rows(slot_rows, weight_rows):
    return lax.dot_general(
        slot_rows, weight_rows, (((1,), (1,)), ((), ())), preferred_element_type=jnp.float32
    )


def local(out_grad, expert_ids, affinity_logits, activations, down_weight):
    tok_rows = out_grad.shape[0]
    feat_width = out_grad.shape[1]
    peer_count = lax.axis_size("expert")
    capacity = tok_rows // 16
    slot_count = peer_count * capacity
    group_size = EXPERTS // peer_count
    affinity = jax.nn.sigmoid(affinity_logits)
    aff_total = jnp.sum(affinity, axis=1, keepdims=True)
    gate_vals = 2.5 * affinity / aff_total
    is_live = expert_ids % group_size == 0
    target = expert_ids // group_size
    experts_row = jnp.arange(peer_count, dtype=jnp.int32)[None, None, :]
    onehot = ((target[:, :, None] == experts_row) & is_live[:, :, None]).astype(jnp.int32)
    per_token = jnp.sum(onehot, axis=1)
    before = jnp.cumsum(per_token, axis=0) - per_token
    ranking = jnp.sum(onehot * before[:, None, :], axis=2)
    slot_key = jnp.where(is_live, target * capacity + ranking, slot_count).reshape(-1)
    token_list = jnp.repeat(jnp.arange(tok_rows, dtype=jnp.int32), TOP)
    source_of = (
        jnp.full((slot_count,), tok_rows, jnp.int32).at[slot_key].set(token_list, mode="drop")
    )
    gate_send = (
        jnp.zeros((slot_count,), jnp.float32).at[slot_key].set(gate_vals.reshape(-1), mode="drop")
    )
    gate_send = gate_send.astype(jnp.bfloat16).reshape(peer_count, capacity)
    padded = jnp.concatenate([out_grad, jnp.zeros((1, feat_width), out_grad.dtype)], axis=0)
    send_rows = padded[source_of].reshape(peer_count, capacity, feat_width)
    slot_rows, gate_in = (
        lax.all_to_all(send_rows, "expert", split_axis=0, concat_axis=0, tiled=True),
        lax.all_to_all(gate_send, "expert", split_axis=0, concat_axis=0, tiled=True),
    )
    slot_rows = slot_rows.reshape(slot_count, feat_width)
    gate_col = gate_in.reshape(slot_count, 1).astype(jnp.float32)
    hidden = activations.reshape(slot_count, activations.shape[-1])
    weight_shard = down_weight[0]
    gathered = lax.all_gather(weight_shard, "dp", axis=0, tiled=True)
    hidden_raw = contract_rows(slot_rows, gathered)
    hidden_grad = (gate_col * hidden_raw).astype(jnp.bfloat16).reshape(activations.shape)
    slot_dgate = jnp.sum(hidden_raw * hidden.astype(jnp.float32), axis=1)
    returned = lax.all_to_all(
        slot_dgate.reshape(peer_count, capacity), "expert", split_axis=0, concat_axis=0, tiled=True
    )
    flat_dgate = jnp.concatenate([returned.reshape(-1), jnp.zeros((1,), jnp.float32)])
    route_dgate = jnp.where(
        is_live, flat_dgate[slot_key].reshape(tok_rows, TOP), jnp.zeros((), jnp.float32)
    )
    mean_term = jnp.sum(route_dgate * affinity, axis=1, keepdims=True) / aff_total
    logit_grad = affinity * (1.0 - affinity) * (2.5 / aff_total) * (route_dgate - mean_term)
    weighted = (gate_col * slot_rows.astype(jnp.float32)).astype(jnp.bfloat16)
    weight_grad = lax.psum_scatter(
        lax.dot_general(
            hidden, weighted, (((0,), (0,)), ((), ())), preferred_element_type=jnp.float32
        ).astype(jnp.bfloat16),
        "dp",
        scatter_dimension=0,
        tiled=True,
    ).astype(jnp.float32)
    return (hidden_grad, weight_grad.reshape(down_weight.shape), logit_grad)


def solution(mesh):
    return jax.shard_map(
        local,
        mesh=mesh,
        in_specs=(
            P(("dp", "expert"), None),
            P(("dp", "expert"), None),
            P(("dp", "expert"), None),
            P("dp", "expert", None, None),
            P("expert", "dp", None),
        ),
        out_specs=(
            P("dp", "expert", None, None),
            P("expert", "dp", None),
            P(("dp", "expert"), None),
        ),
        check_vma=False,
    )
```

profile of v0, /device:TPU:0, one launch (start us, length us, event | category | flops | bytes accessed | tf_op | source)
XLA Modules:
  0.0 239.0 jit_solution(15596274219070694386)
XLA Ops:
  7.2 0.0 copy-start.3
  7.2 0.0 all-gather.3.cloned.1.call-start
  7.2 0.7 all-gather.3.cloned.1.call-update
  7.9 0.0 copy-done.3
  8.0 1.1 reduce-window.6
  9.1 0.2 slice_reduce_fusion
  9.4 0.1 bitcast_subtract_fusion
  9.5 0.1 select_reduce_fusion
  9.6 0.1 copy.36
  9.7 0.2 reshape.144
  9.9 0.1 reshape.187
  10.1 4.2 %concatenate.6 = bf16[513,3584]{1,0:T(8,128)(2,1)} pad(bf16[512,3584]{1,0:T(8,128)(2,1)} %param.5, bf16[]{:T(256)} %constant.53.clone.1), padding=0_1x0_0 | pad | bytes 7347202 | tf_op jit(solution)/shard_map/concatenate | solution.py:42
  14.3 15.5 %scatter_custom_fusion.1 = s32[256]{0:T(256)S(1)} fusion(s32[4096]{0:T(1024)S(1)} %bitcast.36, s32[4096]{0:T(1024)S(1)} %reshape.187, s32[]{:T(128)} %constant.54.clone.1), kind=kCustom, calls=%fused_computation.44 | custom fusion | bytes 1028 | tf_op jit(solution)/shard_map/scatter | solution.py:36
  29.8 6.1 %gather_fusion = bf16[256,3584]{1,0:T(8,128)(2,1)S(1)} fusion(bf16[513,3584]{1,0:T(8,128)(2,1)} %concatenate.6, s32[1024]{0:T(1024)S(1)} %pad_clamp_fusion), kind=kCustom, calls=%fused_computation | custom fusion | bytes 3671040 | tf_op jit(solution)/shard_map/gather | solution.py:43
  35.9 0.0 copy-start.1
  35.9 49.9 %all_to_all.24 = bf16[8,32,3584]{2,1,0:T(8,128)(2,1)} all-to-all(bf16[8,32,3584]{2,1,0:T(8,128)(2,1)S(1)} %bitcast.32), channel_id=1, replica_groups=mesh['dp'=4,'expert'=8] {'expert'}, dimensions={0} | all-to-all | bytes 3670016 | tf_op jit(solution)/shard_map/all_to_all | solution.py:45
  85.9 0.0 all-gather.3.cloned.1.call-done
  85.9 0.0 copy-done.1
  85.9 5.8 %multiply_reduce_fusion = (f32[256]{0:T(256)S(1)}, f32[256,1024]{1,0:T(8,128)S(1)}) fusion(bf16[1,1,256,1024]{3,2,1,0:T(8,128)(2,1)S(1)} %copy-done.1, bf16[256,3584]{1,0:T(8,128)(2,1)} %bitcast.33, bf16[1,1024,3584]{2,1,0:T(8,128)(2,1)} %all-gather.3.cloned.1.call-done), kind=kOutput, calls=%fused_computation.10 | convolution fusion | flops 1879834368 | bytes 10748928 | tf_op jit(solution)/shard_map/dot_general | solution.py:11
  91.7 0.7 all_to_all.18
  92.4 3.6 %all-to-all-start.2 = ((f32[8,1,32]{2,1,0:T(1,128)}), f32[8,1,32]{2,1,0:T(1,128)S(1)}, u32[]{:S(2)}, u32[]{:S(2)}) async-start(f32[8,1,32]{2,1,0:T(1,128)} %all_to_all.18), calls=%async_computation.3 | async-start | bytes 8192 | tf_op jit(solution)/shard_map/all_to_all | solution.py:56
  96.0 0.0 reduce-scatter.2.cloned.1.call-start
  96.0 6.4 %all-to-all-done.2 = f32[8,1,32]{2,1,0:T(1,128)S(1)} async-done(((f32[8,1,32]{2,1,0:T(1,128)}), f32[8,1,32]{2,1,0:T(1,128)S(1)}, u32[]{:S(2)}, u32[]{:S(2)}) %all-to-all-start.2) | async-done | bytes 1056 | tf_op jit(solution)/shard_map/all_to_all | solution.py:56
  102.4 0.5 broadcast.105
  102.9 0.7 reduce.9
  103.6 0.1 reshape.153
  103.7 0.0 copy-start.4
  103.7 0.0 copy-start
  103.7 25.9 %gather_fusion.1 = f32[4096]{0:T(1024)S(1)} fusion(f32[257]{0:T(512)S(1)} %pad_maximum_fusion, s32[4096]{0:T(1024)S(1)} %broadcast_clamp_fusion), kind=kCustom, calls=%fused_computation.1 | custom fusion | bytes 49152 | tf_op jit(solution)/shard_map/gather | solution.py:61
  129.6 0.2 reshape.154
  129.7 0.1 copy.39
  129.8 0.0 copy-done.4
  129.9 0.6 fusion.8
  130.5 0.1 copy.37
  130.6 0.2 reshape.179
  130.8 15.5 %scatter_custom_fusion = f32[256]{0:T(256)S(1)} fusion(s32[4096]{0:T(1024)S(1)} %bitcast.37, f32[4096]{0:T(1024)S(1)} %reshape.179, f32[]{:T(128)} %constant.19.clone.1), kind=kCustom, calls=%fused_computation.46 | custom fusion | bytes 1028 | tf_op jit(solution)/shard_map/scatter | solution.py:39
  146.3 0.1 all_to_all.20
  146.4 8.8 %all_to_all.25 = bf16[8,1,32]{2,1,0:T(2,128)(2,1)S(1)} all-to-all(bf16[8,1,32]{2,1,0:T(2,128)(2,1)S(1)} %all_to_all.20), channel_id=1, replica_groups=mesh['dp'=4,'expert'=8] {'expert'}, dimensions={0} | all-to-all | bytes 1024 | tf_op jit(solution)/shard_map/all_to_all | solution.py:46
  155.2 0.0 copy-done
  155.3 0.0 copy-start.2
  155.3 0.5 multiply_convert_fusion
  155.7 0.6 copy-done.2
  156.3 5.1 %fusion.2 = bf16[1024,3584]{0,1:T(8,128)(2,1)} fusion(bf16[256,3584]{1,0:T(8,128)(2,1)S(1)} %bitcast.31, bf16[1,1,256,1024]{3,2,1,0:T(8,128)(2,1)S(1)} %copy-done.2), kind=kOutput, calls=%fused_computation.7 | convolution fusion | flops 1882718208 | bytes 9699328 | tf_op jit(solution)/shard_map/dot_general | solution.py:67
  161.4 0.0 reduce-scatter.2.cloned.1.call-update
  161.4 0.1 reshape.155
  161.5 0.9 fusion.3
  162.4 61.1 %reduce-scatter.2.cloned.1.call-done = bf16[256,3584]{0,1:T(8,128)(2,1)} async-done(((bf16[1024,3584]{0,1:T(8,128)(2,1)}), bf16[256,3584]{0,1:T(8,128)(2,1)}) %reduce-scatter.2.cloned.1.call-update) | async-done | bytes 1835024 | tf_op jit(solution)/shard_map/reduce_scatter | solution.py:66
  223.5 3.6 %bitcast_convert_fusion = f32[1,256,3584]{1,2,0:T(8,128)} fusion(bf16[256,3584]{0,1:T(8,128)(2,1)} %reduce-scatter.2.cloned.1.call-done), kind=kLoop, calls=%fused_computation.9 | loop fusion | flops 917504 | bytes 5505024 | tf_op jit(solution)/shard_map/reshape | solution.py:74
  227.1 5.1 %copy.40 = f32[1,256,3584]{2,1,0:T(8,128)} copy(f32[1,256,3584]{1,2,0:T(8,128)} %bitcast_convert_fusion) | data formatting | bytes 7340032
  (17 shorter events, 0.3 us)
Async XLA Ops:
  7.2 0.7 copy-start.3
  7.2 78.7 %all-gather.3.cloned.1.call-start = ((), (), s32[]{:S(2)}) async-start(), calls=%async_computation.5 | async-start | bytes 9175040 | tf_op jit(solution)/shard_map/all_gather | solution.py:52
  35.9 49.9 %copy-start.1 = (bf16[1,1,256,1024]{3,2,1,0:T(8,128)(2,1)S(1)}, bf16[1,1,256,1024]{3,2,1,0:T(8,128)(2,1)}, u32[]{:S(2)}) copy-start(bf16[1,1,256,1024]{3,2,1,0:T(8,128)(2,1)} %param.8) | copy-start | bytes 1572868
  92.4 10.0 %all-to-all-start.2 = ((f32[8,1,32]{2,1,0:T(1,128)}), f32[8,1,32]{2,1,0:T(1,128)S(1)}, u32[]{:S(2)}, u32[]{:S(2)}) async-start(f32[8,1,32]{2,1,0:T(1,128)} %all_to_all.18), calls=%async_computation.3 | async-start | bytes 8192 | tf_op jit(solution)/shard_map/all_to_all | solution.py:56
  96.0 127.5 %reduce-scatter.2.cloned.1.call-start = ((), (), s32[]{:S(2)}) async-start(), calls=%async_computation.4 | async-start | bytes 9175040 | tf_op jit(solution)/shard_map/reduce_scatter | solution.py:66
  103.7 26.2 %copy-start.4 = (f32[512,8]{0,1:T(8,128)S(1)}, f32[512,8]{0,1:T(8,128)}, u32[]{:S(2)}) copy-start(f32[512,8]{0,1:T(8,128)} %param.7) | copy-start | bytes 49156
  103.7 51.6 %copy-start = (bf16[8,32,3584]{2,1,0:T(8,128)(2,1)S(1)}, bf16[8,32,3584]{2,1,0:T(8,128)(2,1)}, u32[]{:S(2)}) copy-start(bf16[8,32,3584]{2,1,0:T(8,128)(2,1)} %all_to_all.24) | copy-start | bytes 5505028
  155.3 1.0 copy-start.2
Sparse Core Ops, SparseCore 0:
  9.5 55.0 all-gather.2
  161.5 61.9 reduce-scatter.1
where the time goes:
time: 240 us; the launch traced here: 239 us
  local copies, waits for them, and re-layouts  75.5 us (31%)
  waiting for transfers between devices  68.1 us (28%)
  blocking collectives  58.8 us (24%)
  between operations  14.3 us (6%)
  matrix products  10.9 us (5%)
  other arithmetic  7.79 us (3%)
  starting transfers between devices  3.67 us (2%)
    reduce_scatter x1, waiting for transfers between devices, local(): lax.psum_scatter(lax.dot_general(hidden, weighted, (((0,), (0,)), ((), ()...  61.1 us
    all_to_all x1, blocking collectives, local(): lax.all_to_all(send_rows, 'expert', split_axis=0, concat_axis=0, tiled=True)  49.9 us
    gather x1, local copies, waits for them, and re-layouts, local(): flat_dgate[slot_key].reshape(tok_rows, TOP)  25.9 us
    scatter x1, local copies, waits for them, and re-layouts, local(): jnp.full((slot_count,), tok_rows, jnp.int32).at[slot_key]  15.5 us
    scatter x1, local copies, waits for them, and re-layouts, local(): jnp.zeros((slot_count,), jnp.float32).at[slot_key]  15.5 us
    all_to_all x1, blocking collectives, local(): lax.all_to_all(gate_send, 'expert', split_axis=0, concat_axis=0, tiled=True)  8.85 us
    all_to_all x1, waiting for transfers between devices, local(): lax.all_to_all(slot_dgate.reshape(peer_count, capacity), 'expert', split_...  6.36 us
    gather x1, local copies, waits for them, and re-layouts, local(): send_rows = padded[source_of].reshape(peer_count, capacity, feat_width)  6.07 us
  transfers between devices with their start and end apart: 3, of which 2 were waited for; matrix products, arithmetic and copies ran while one was open for 12% of the time, Pallas kernels for 0%

commit v1 on v0

--- a/solution.py
+++ b/solution.py
@@ -1,6 +1,10 @@
+import functools
+
 import jax
 import jax.numpy as jnp
 from jax import lax
+from jax.experimental import pallas as pl
+from jax.experimental.pallas import tpu as pltpu
 from jax.sharding import PartitionSpec as P
 
 EXPERTS = 256
@@ -13,7 +17,7 @@
     )
 
 
-def local(out_grad, expert_ids, affinity_logits, activations, down_weight):
+def local_native(out_grad, expert_ids, affinity_logits, activations, down_weight):
     tok_rows = out_grad.shape[0]
     feat_width = out_grad.shape[1]
     peer_count = lax.axis_size("expert")
@@ -74,9 +78,285 @@
     return (hidden_grad, weight_grad.reshape(down_weight.shape), logit_grad)
 
 
+MESH = pl.DeviceIdType.MESH
+VMEM_BUDGET = 60 * 1024 * 1024
+
+
+def flip(index, mask):
+    out, bit = index, 1
+    while bit <= mask:
+        if mask & bit:
+            out = out + bit * (1 - 2 * lax.rem(lax.div(index, bit), 2))
+        bit *= 2
+    return out
+
+
+def mm(a, b, dims):
+    return lax.dot_general(a, b, (dims, ((), ())), preferred_element_type=jnp.float32)
+
+
+NN, NT = ((1,), (0,)), ((1,), (1,))
+
+
+def kernel(
+    n_dp, n_e, cap, block,
+    ids_ref, logit_ref, og_ref, act_ref, w_ref,
+    hid_ref, wg_ref, lg_ref,
+    packed, rows, actb, act_t, hacc, hsend, hbuf, dsend, drecv,
+    a_send, a_recv, y_send, y_recv, s_send, s_recv, f_send, f_recv,
+    act_send, act_recv, h_send, h_recv, d_send, d_recv,
+):
+    me = lax.axis_index("dp")
+    ex = lax.axis_index("expert")
+    sib, ypart = flip(me, 1), flip(me, 2)
+    toks, width = og_ref.shape
+    shard = w_ref.shape[0]
+    slots = n_e * cap
+    half = n_e // 2
+    part = half * cap
+    blocks = width // block
+    my_cols = pl.ds(pl.multiple_of(me * shard, shard), shard)
+    group = EXPERTS // n_e
+
+    barrier = pltpu.get_barrier_semaphore()
+    for m in range(1, n_e):
+        pl.semaphore_signal(barrier, inc=1, device_id={"expert": flip(ex, m)}, device_id_type=MESH)
+    for k in range(1, n_dp):
+        pl.semaphore_signal(barrier, inc=1, device_id={"dp": flip(me, k)}, device_id_type=MESH)
+
+    ids = ids_ref[0:1, :]
+    live = lax.rem(ids, group) == 0
+    target = lax.div(ids, group)
+    e_iota = lax.broadcasted_iota(jnp.int32, (n_e, toks), 0)
+    chosen = jnp.where((target == e_iota) & live, 1.0, 0.0)
+    earlier = jnp.where(
+        lax.broadcasted_iota(jnp.int32, (toks, toks), 0)
+        < lax.broadcasted_iota(jnp.int32, (toks, toks), 1), 1.0, 0.0
+    ).astype(jnp.bfloat16)
+    before = mm(chosen.astype(jnp.bfloat16), earlier, NN)
+    rank = jnp.sum(chosen * before, axis=0, keepdims=True).astype(jnp.int32)
+    aff = 1.0 / (1.0 + jnp.exp(-logit_ref[...]))
+    total = jnp.sum(aff, axis=0, keepdims=True)
+    gate = (2.5 * aff[0:1, :] / total).astype(jnp.bfloat16).astype(jnp.float32)
+    slot = jnp.where(live, target * cap + rank, -1)
+    s_iota = lax.broadcasted_iota(jnp.int32, (slots, toks), 0)
+    place = jnp.where(s_iota == slot, gate, 0.0).astype(jnp.bfloat16)
+
+    def pack(b, carry):
+        cols = pl.ds(pl.multiple_of(b * block, block), block)
+        got = mm(place, og_ref[:, cols], NN).astype(jnp.bfloat16)
+        packed[:, :, cols] = got.reshape(n_e, cap, block)
+        return carry
+
+    lax.fori_loop(0, blocks, pack, 0)
+    pl.semaphore_wait(barrier, n_e - 1 + n_dp - 1)
+
+    def remote(src, dst, send, recv, where):
+        copy = pltpu.make_async_remote_copy(
+            src_ref=src, dst_ref=dst, send_sem=send, recv_sem=recv,
+            device_id=where, device_id_type=MESH,
+        )
+        copy.start()
+        return copy
+
+    own_copies, y_copies, s_copies, f_copies, sent = {}, {}, {}, {}, []
+
+    def own_step(m):
+        src_of = flip(ex, m)
+        if m:
+            own_copies[m].wait_recv()
+        source = packed.at[ex] if m == 0 else rows.at[me, src_of]
+        y_copies[m] = remote(source, rows.at[me, src_of], y_send.at[m], y_recv.at[m], {"dp": ypart})
+        s_copies[m] = remote(source, rows.at[me, src_of], s_send.at[m], s_recv.at[m], {"dp": sib})
+
+    def y_step(m):
+        src_of = flip(ex, m)
+        y_copies[m].wait_recv()
+        f_copies[m] = remote(
+            rows.at[ypart, src_of], rows.at[ypart, src_of], f_send.at[m], f_recv.at[m], {"dp": sib}
+        )
+
+    for m in [1] + list(range(half, n_e)) + list(range(2, half)):
+        peer = flip(ex, m)
+        own_copies[m] = remote(
+            packed.at[peer], rows.at[me, ex], a_send.at[m], a_recv.at[m], {"expert": peer}
+        )
+    own_step(0)
+    act_copies = []
+    for k in range(1, n_dp):
+        peer = flip(me, k)
+        theirs = pl.ds(pl.multiple_of(peer * shard, shard), shard)
+        act_copies.append(remote(
+            act_ref.at[:, theirs], actb.at[me], act_send.at[k], act_recv.at[k], {"dp": peer}
+        ))
+    rows[me, ex] = packed[ex]
+    actb[me] = act_ref[:, my_cols]
+
+    h_copies = {}
+
+    def arrived(g):
+        for m in range(g * half, (g + 1) * half):
+            s_copies[m].wait_recv()
+            f_copies[m].wait_recv()
+
+    def group_start(g):
+        first = lax.div(ex, half)
+        return (first if g == 0 else 1 - first) * half
+
+    def rows_block(g, cols):
+        got = rows[:, pl.ds(group_start(g), half), :, cols]
+        return got.reshape(n_dp * part, block)
+
+    def hidden_part(g):
+        hacc[...] = jnp.zeros_like(hacc)
+
+        def step(b, carry):
+            cols = pl.ds(pl.multiple_of(b * block, block), block)
+            hacc[...] += mm(rows_block(g, cols), w_ref[:, cols], NT)
+            return carry
+
+        lax.fori_loop(0, blocks, step, 0)
+        hsend[g] = hacc[...].astype(jnp.bfloat16).reshape(n_dp, part, shard)
+        at = pl.ds(pl.multiple_of(group_start(g) * cap, part), part)
+        for k in range(1, n_dp):
+            peer = flip(me, k)
+            h_copies[g, k] = remote(
+                hsend.at[g, peer], hbuf.at[at, my_cols], h_send.at[g, k], h_recv.at[g, k], {"dp": peer}
+            )
+        hbuf[at, my_cols] = hsend[g, me]
+
+    def grad_part(g):
+        at = pl.ds(pl.multiple_of(group_start(g) * cap, part), part)
+        act_t[...] = actb[:, at, :].reshape(n_dp * part, shard).T
+
+        def step(b, carry):
+            cols = pl.ds(pl.multiple_of(b * block, block), block)
+            term = mm(act_t[...], rows_block(g, cols), NN)
+            wg_ref[:, cols] = term if g == 0 else wg_ref[:, cols] + term
+            return carry
+
+        lax.fori_loop(0, blocks, step, 0)
+
+    lag = 1
+    for m in range(1, n_e):
+        own_step(m)
+        y_step(m - lag)
+        if m == half + 1:
+            for copy in act_copies:
+                copy.wait_recv()
+            arrived(0)
+            hidden_part(0)
+            grad_part(0)
+    y_step(n_e - 1)
+    arrived(1)
+    hidden_part(1)
+    grad_part(1)
+
+    for g in range(2):
+        for k in range(1, n_dp):
+            h_copies[g, k].wait_recv()
+    hid_ref[...] = hbuf[...]
+    ones = jnp.ones((8, shard), jnp.bfloat16)
+    dots = jnp.zeros((8, slots), jnp.float32)
+    for j in range(n_dp):
+        cols = slice(j * shard, (j + 1) * shard)
+        prod = hbuf[:, cols].astype(jnp.float32) * act_ref[:, cols].astype(jnp.float32)
+        high = prod.astype(jnp.bfloat16)
+        low = (prod - high.astype(jnp.float32)).astype(jnp.bfloat16)
+        dots = dots + mm(ones, high, NT) + mm(ones, low, NT)
+    dsend[...] = dots[0:1, :]
+    d_copies = []
+    for m in range(1, n_e):
+        d_copies.append(remote(
+            dsend, drecv.at[ex], d_send.at[m], d_recv.at[m], {"expert": flip(ex, m)}
+        ))
+    drecv[ex] = dots[0:1, :]
+    pick = jnp.where((s_iota == ex * cap + rank) & live, 1.0, 0.0).astype(jnp.bfloat16)
+    for copy in d_copies:
+        copy.wait_recv()
+    rest = drecv[...].reshape(n_e, slots)
+    looked = jnp.zeros((n_e, toks), jnp.float32)
+    for _ in range(3):
+        piece = rest.astype(jnp.bfloat16)
+        looked = looked + mm(piece, pick, NN)
+        rest = rest - piece.astype(jnp.float32)
+    route = jnp.sum(chosen * looked, axis=0, keepdims=True)
+    route = jnp.where(live, route / gate, 0.0)
+    mean = route * aff[0:1, :] / total
+    k_iota = lax.broadcasted_iota(jnp.int32, aff.shape, 0)
+    lg_ref[...] = aff * (1.0 - aff) * (2.5 / total) * (jnp.where(k_iota == 0, route, 0.0) - mean)
+
+    for copies in (own_copies, y_copies, s_copies, f_copies, h_copies):
+        for copy in copies.values():
+            copy.wait_send()
+    for copy in act_copies + d_copies:
+        copy.wait_send()
+
+
+def local(sizes, out_grad, expert_ids, affinity_logits, activations, down_weight):
+    n_dp, n_e = sizes["dp"], sizes["expert"]
+    toks, width = out_grad.shape
+    cap = toks // 16
+    slots = n_e * cap
+    hidden_width = activations.shape[-1]
+    shard = down_weight.shape[1]
+    block = 512
+    part = slots // 2
+    bf16, f32 = jnp.bfloat16, jnp.float32
+    row_bytes = 2 * width
+    need = (
+        toks * row_bytes + slots * row_bytes + n_dp * slots * row_bytes + shard * row_bytes * 3
+        + slots * hidden_width * 8 + n_dp * slots * shard * 8 + toks * toks * 8
+    )
+    fits = (
+        n_dp == 4 and n_e >= 4 and n_e & (n_e - 1) == 0 and need < VMEM_BUDGET
+        and width % block == 0 and shard % 128 == 0 and (EXPERTS // n_e) % TOP == 0
+    )
+    if not fits:
+        return local_native(out_grad, expert_ids, affinity_logits, activations, down_weight)
+    vmem = pl.BlockSpec(memory_space=pltpu.VMEM)
+    dma = pltpu.SemaphoreType.DMA
+    hidden_grad, weight_grad, logit_t = pl.pallas_call(
+        functools.partial(kernel, n_dp, n_e, cap, block),
+        out_shape=(
+            jax.ShapeDtypeStruct((slots, hidden_width), bf16),
+            jax.ShapeDtypeStruct((shard, width), f32),
+            jax.ShapeDtypeStruct((TOP, toks), f32),
+        ),
+        in_specs=[vmem] * 5,
+        out_specs=(vmem,) * 3,
+        scratch_shapes=[
+            pltpu.VMEM((n_e, cap, width), bf16),
+            pltpu.VMEM((n_dp, n_e, cap, width), bf16),
+            pltpu.VMEM((n_dp, slots, shard), bf16),
+            pltpu.VMEM((shard, n_dp * part), bf16),
+            pltpu.VMEM((n_dp * part, shard), f32),
+            pltpu.VMEM((2, n_dp, part, shard), bf16),
+            pltpu.VMEM((slots, hidden_width), bf16),
+            pltpu.VMEM((1, slots), f32),
+            pltpu.VMEM((n_e, 1, slots), f32),
+            dma((n_e,)), dma((n_e,)), dma((n_e,)), dma((n_e,)),
+            dma((n_e,)), dma((n_e,)), dma((n_e,)), dma((n_e,)),
+            dma((n_dp,)), dma((n_dp,)), dma((2, n_dp)), dma((2, n_dp)),
+            dma((n_e,)), dma((n_e,)),
+        ],
+        compiler_params=pltpu.CompilerParams(
+            collective_id=0, has_side_effects=True, vmem_limit_bytes=VMEM_BUDGET
+        ),
+    )(
+        expert_ids.T, affinity_logits.T, out_grad,
+        activations.reshape(slots, hidden_width), down_weight[0],
+    )
+    return (
+        hidden_grad.reshape(activations.shape),
+        weight_grad.reshape(down_weight.shape),
+        logit_t.T,
+    )
+
+
 def solution(mesh):
     return jax.shard_map(
-        local,
+        functools.partial(local, dict(mesh.shape)),
         mesh=mesh,
         in_specs=(
             P(("dp", "expert"), None),

time: 240 us -> 91.2 us (0.38)
  Pallas kernels: 0 us -> 83.7 us
  local copies, waits for them, and re-layouts: 75.5 us -> 6.61 us
  waiting for transfers between devices: 68.1 us -> 0 us
  blocking collectives: 58.8 us -> 0 us
  between operations: 14.3 us -> 0.64 us
  matrix products: 10.9 us -> 0 us
  other arithmetic: 7.79 us -> 0 us
  starting transfers between devices: 3.67 us -> 0 us
    pallas_call x0 -> x1, Pallas kernels: none -> 83.7 us  [local(): pl.pallas_call(functools.partial(kernel, n_dp, n_e, cap, block), out_shap...]
    reduce_scatter x1 -> x0, waiting for transfers between devices: 61.1 us -> none  [local(): lax.psum_scatter(lax.dot_general(hidden, weighted, (((0,), (0,)), ((), ()...]
    all_to_all x2 -> x0, blocking collectives: 58.8 us -> none  [the longest x1 49.9 us: local(): lax.all_to_all(send_rows, 'expert', split_axis=0, concat_axis=0, tiled=True)]
    gather x2 -> x0, local copies, waits for them, and re-layouts: 31.9 us -> none  [the longest x1 25.9 us: local(): flat_dgate[slot_key].reshape(tok_rows, TOP)]
    scatter x2 -> x0, local copies, waits for them, and re-layouts: 31 us -> none  [the longest x1 15.5 us: local(): jnp.full((slot_count,), tok_rows, jnp.int32).at[slot_key]]
    dot_general x2 -> x0, matrix products: 10.9 us -> none  [the longest x1 5.82 us: contract_rows(): lax.dot_general(slot_rows, weight_rows, (((1,), (1,)), ((), ())), preferr...]
    all_to_all x1 -> x0, waiting for transfers between devices: 6.36 us -> none  [local(): lax.all_to_all(slot_dgate.reshape(peer_count, capacity), 'expert', split_...]
    reshape x2 -> x0, other arithmetic: 4.5 us -> none  [the longest x1 3.58 us: local(): return (hidden_grad, weight_grad.reshape(down_weight.shape), logit_grad)]
  transfers between devices with their start and end apart: 3 -> 0, of which waited for: 2 -> 0; matrix products, arithmetic and copies ran while one was open for 12% -> 0% of each run, Pallas kernels for 0% -> 0%
where the time goes in v1:
time: 91.2 us; the launch traced here: 91 us
  Pallas kernels  83.7 us (92%)
  local copies, waits for them, and re-layouts  6.61 us (7%)
    pallas_call x1, Pallas kernels, local(): pl.pallas_call(functools.partial(kernel, n_dp, n_e, cap, block), out_shap...  83.7 us
    unnamed x5, local copies, waits for them, and re-layouts  6.61 us

profile of v1, /device:TPU:0, one launch (start us, length us, event | category | flops | bytes accessed | tf_op | source)
XLA Modules:
  0.0 91.0 jit_solution(12062631828448050288)
XLA Ops:
  0.6 83.7 %shard_map.76 = (bf16[256,1024]{1,0:T(8,128)(2,1)}, f32[256,3584]{1,0:T(8,128)}, f32[8,512]{1,0:T(8,128)}) custom-call(s32[8,512]{1,0:T(8,128)} %bitcast.11, f32[8,512]{1,0:T(8,128)} %bitcast.12, bf16[512,3584]{1,0:T(8,128)(2,1)} %og_ref.1, bf16[256,1024]{1,0:T(8,128)(2,1)} %bitcast.9, bf16[256,3584]{1,0:T(8,128)(2,1)} %bitcast.8), custom_call_target="tpu_custom_call" | custom-call | tf_op jit(solution)/shard_map/pallas_call | solution.py:319
  84.4 1.9 %copy.11 = bf16[1,1,256,1024]{3,2,1,0:T(8,128)(2,1)} copy(bf16[1,1,256,1024]{3,2,1,0:T(8,128)(2,1)} %bitcast.10) | data formatting | bytes 1048576
  86.2 0.0 copy-start
  86.2 4.1 %copy.12 = f32[1,256,3584]{2,1,0:T(8,128)} copy(f32[1,256,3584]{2,1,0:T(8,128)} %bitcast.7) | data formatting | bytes 7340032
  90.4 0.0 copy-done
  90.4 0.6 copy.13
Async XLA Ops:
  86.2 4.1 %copy-start = (f32[8,512]{1,0:T(8,128)S(1)}, f32[8,512]{1,0:T(8,128)}, u32[]{:S(2)}) copy-start(f32[8,512]{1,0:T(8,128)} %get-tuple-element.8) | copy-start | bytes 49156

commit v2 on v1

--- a/solution.py
+++ b/solution.py
@@ -79,7 +79,7 @@
 
 
 MESH = pl.DeviceIdType.MESH
-VMEM_BUDGET = 60 * 1024 * 1024
+VMEM_ALL = 67043328
 
 
 def flip(index, mask):
@@ -100,11 +100,11 @@
 
 def kernel(
     n_dp, n_e, cap, block,
-    ids_ref, logit_ref, og_ref, act_ref, w_ref,
+    ids_ref, logit_ref, og_hbm, act_hbm, w_hbm,
     hid_ref, wg_ref, lg_ref,
-    packed, rows, actb, act_t, hacc, hsend, hbuf, dsend, drecv,
-    a_send, a_recv, y_send, y_recv, s_send, s_recv, f_send, f_recv,
-    act_send, act_recv, h_send, h_recv, d_send, d_recv,
+    og_ref, act_ref, w_ref, packed, stage, rows, actb, act_t, hacc, hsend, hbuf, dsend, drecv,
+    load_sem, w_sem, a_send, a_recv, y_send, y_recv, s_send, s_recv, f_send, f_recv,
+    r_send, r_recv, act_send, act_recv, h_send, h_recv, d_send, d_recv,
 ):
     me = lax.axis_index("dp")
     ex = lax.axis_index("expert")
@@ -112,11 +112,25 @@
     toks, width = og_ref.shape
     shard = w_ref.shape[0]
     slots = n_e * cap
-    half = n_e // 2
-    part = half * cap
+    quarter = n_e // 4
     blocks = width // block
     my_cols = pl.ds(pl.multiple_of(me * shard, shard), shard)
     group = EXPERTS // n_e
+
+    def block_cols(b):
+        return pl.ds(pl.multiple_of(b * block, block), block)
+
+    def load(b):
+        return pltpu.make_async_copy(
+            og_hbm.at[:, block_cols(b)], og_ref.at[:, block_cols(b)], load_sem.at[b]
+        )
+
+    for b in range(blocks):
+        load(b).start()
+    act_load = pltpu.make_async_copy(act_hbm, act_ref, w_sem.at[0])
+    act_load.start()
+    w_load = pltpu.make_async_copy(w_hbm, w_ref, w_sem.at[1])
+    w_load.start()
 
     barrier = pltpu.get_barrier_semaphore()
     for m in range(1, n_e):
@@ -142,13 +156,7 @@
     s_iota = lax.broadcasted_iota(jnp.int32, (slots, toks), 0)
     place = jnp.where(s_iota == slot, gate, 0.0).astype(jnp.bfloat16)
 
-    def pack(b, carry):
-        cols = pl.ds(pl.multiple_of(b * block, block), block)
-        got = mm(place, og_ref[:, cols], NN).astype(jnp.bfloat16)
-        packed[:, :, cols] = got.reshape(n_e, cap, block)
-        return carry
-
-    lax.fori_loop(0, blocks, pack, 0)
+    act_load.wait()
     pl.semaphore_wait(barrier, n_e - 1 + n_dp - 1)
 
     def remote(src, dst, send, recv, where):
@@ -159,100 +167,158 @@
         copy.start()
         return copy
 
-    own_copies, y_copies, s_copies, f_copies, sent = {}, {}, {}, {}, []
-
-    def own_step(m):
-        src_of = flip(ex, m)
-        if m:
-            own_copies[m].wait_recv()
-        source = packed.at[ex] if m == 0 else rows.at[me, src_of]
-        y_copies[m] = remote(source, rows.at[me, src_of], y_send.at[m], y_recv.at[m], {"dp": ypart})
-        s_copies[m] = remote(source, rows.at[me, src_of], s_send.at[m], s_recv.at[m], {"dp": sib})
-
-    def y_step(m):
-        src_of = flip(ex, m)
-        y_copies[m].wait_recv()
-        f_copies[m] = remote(
-            rows.at[ypart, src_of], rows.at[ypart, src_of], f_send.at[m], f_recv.at[m], {"dp": sib}
-        )
-
-    for m in [1] + list(range(half, n_e)) + list(range(2, half)):
-        peer = flip(ex, m)
-        own_copies[m] = remote(
-            packed.at[peer], rows.at[me, ex], a_send.at[m], a_recv.at[m], {"expert": peer}
-        )
-    own_step(0)
     act_copies = []
-    for k in range(1, n_dp):
+    for k in range(n_dp - 1, 0, -1):
         peer = flip(me, k)
         theirs = pl.ds(pl.multiple_of(peer * shard, shard), shard)
         act_copies.append(remote(
             act_ref.at[:, theirs], actb.at[me], act_send.at[k], act_recv.at[k], {"dp": peer}
         ))
+
+    def pack(b, carry):
+        load(b).wait()
+        cols = block_cols(b)
+        got = mm(place, og_ref[:, cols], NN).astype(jnp.bfloat16)
+        packed[:, :, cols] = got.reshape(n_e, cap, block)
+        return carry
+
+    lax.fori_loop(0, blocks, pack, 0)
+
+    quad, low = lax.div(ex, quarter), lax.rem(ex, quarter)
+    odd, top = lax.rem(quad, 2), lax.div(quad, 2)
+    inner = lax.rem(odd + top, 2)
+    across, mirror = quad + 2 - 4 * top, 3 - quad
+    quads = [
+        quad, quad + 1 - 2 * odd,
+        mirror + inner * (across - mirror), across + inner * (mirror - across),
+    ]
+    kinds = [0, 1, 3 - inner, 2 + inner]
+
+    def source_of(i):
+        return quads[i // quarter] * quarter + flip(low, i % quarter)
+
+    own_copies, y_copies, s_copies, f_copies, r_copies, h_copies = {}, {}, {}, {}, {}, {}
+
+    near = 2 * quarter
+
+    def own_step(i):
+        src_of = source_of(i)
+        if i:
+            own_copies[i].wait_recv()
+        source = packed.at[ex] if i == 0 else rows.at[me, src_of]
+        if i == 0 or i >= near:
+            y_copies[i] = remote(source, rows.at[me, src_of], y_send.at[i], y_recv.at[i], {"dp": ypart})
+        s_copies[i] = remote(source, rows.at[me, src_of], s_send.at[i], s_recv.at[i], {"dp": sib})
+
+    def relay_step(i):
+        y_copies[i].wait_recv()
+        r_copies[i] = remote(
+            stage.at[i], rows.at[ypart, ex], r_send.at[i], r_recv.at[i], {"expert": source_of(i)}
+        )
+
+    def pass_step(i):
+        src_of = source_of(i)
+        (r_copies if 0 < i < near else y_copies)[i].wait_recv()
+        f_copies[i] = remote(
+            rows.at[ypart, src_of], rows.at[ypart, src_of], f_send.at[i], f_recv.at[i], {"dp": sib}
+        )
+
+    own_step(0)
+    for i in range(1, near):
+        y_copies[i] = remote(
+            packed.at[source_of(i)], stage.at[i], y_send.at[i], y_recv.at[i], {"dp": ypart}
+        )
+    for i in list(range(1, quarter)) + list(range(near, n_e)) + list(range(quarter, near)):
+        peer = source_of(i)
+        at = kinds[i // quarter] * quarter + i % quarter
+        own_copies[i] = remote(
+            packed.at[peer], rows.at[me, ex], a_send.at[at], a_recv.at[at], {"expert": peer}
+        )
     rows[me, ex] = packed[ex]
     actb[me] = act_ref[:, my_cols]
 
-    h_copies = {}
+    groups = [
+        (top * 2 * quarter, 2 * quarter, range(2 * quarter)),
+        (quads[2] * quarter, quarter, range(2 * quarter, 3 * quarter)),
+        (quads[3] * quarter, quarter, range(3 * quarter, n_e)),
+    ]
 
     def arrived(g):
-        for m in range(g * half, (g + 1) * half):
-            s_copies[m].wait_recv()
-            f_copies[m].wait_recv()
-
-    def group_start(g):
-        first = lax.div(ex, half)
-        return (first if g == 0 else 1 - first) * half
+        for i in groups[g][2]:
+            s_copies[i].wait_recv()
+            f_copies[i].wait_recv()
+
+    def span(g):
+        start, count, _ = groups[g]
+        return pl.ds(pl.multiple_of(start * cap, count * cap), count * cap), count * cap
 
     def rows_block(g, cols):
-        got = rows[:, pl.ds(group_start(g), half), :, cols]
-        return got.reshape(n_dp * part, block)
+        start, count, _ = groups[g]
+        return rows[:, pl.ds(start, count), :, cols].reshape(n_dp * count * cap, block)
 
     def hidden_part(g):
-        hacc[...] = jnp.zeros_like(hacc)
+        at, extent = span(g)
+        acc = hacc.at[pl.ds(0, n_dp * extent)]
+        acc[...] = jnp.zeros_like(acc)
 
         def step(b, carry):
-            cols = pl.ds(pl.multiple_of(b * block, block), block)
-            hacc[...] += mm(rows_block(g, cols), w_ref[:, cols], NT)
+            cols = block_cols(b)
+            acc[...] += mm(rows_block(g, cols), w_ref[:, cols], NT)
             return carry
 
         lax.fori_loop(0, blocks, step, 0)
-        hsend[g] = hacc[...].astype(jnp.bfloat16).reshape(n_dp, part, shard)
-        at = pl.ds(pl.multiple_of(group_start(g) * cap, part), part)
-        for k in range(1, n_dp):
+        hsend[:, at, :] = acc[...].astype(jnp.bfloat16).reshape(n_dp, extent, shard)
+        for k in range(n_dp - 1, 0, -1):
             peer = flip(me, k)
             h_copies[g, k] = remote(
-                hsend.at[g, peer], hbuf.at[at, my_cols], h_send.at[g, k], h_recv.at[g, k], {"dp": peer}
+                hsend.at[peer, at], hbuf.at[at, my_cols], h_send.at[g, k], h_recv.at[g, k], {"dp": peer}
             )
-        hbuf[at, my_cols] = hsend[g, me]
+        hbuf[at, my_cols] = hsend[me, at, :]
 
     def grad_part(g):
-        at = pl.ds(pl.multiple_of(group_start(g) * cap, part), part)
-        act_t[...] = actb[:, at, :].reshape(n_dp * part, shard).T
+        at, extent = span(g)
+        lhs = act_t.at[:, pl.ds(0, n_dp * extent)]
+        lhs[...] = actb[:, at, :].reshape(n_dp * extent, shard).T
 
         def step(b, carry):
-            cols = pl.ds(pl.multiple_of(b * block, block), block)
-            term = mm(act_t[...], rows_block(g, cols), NN)
+            cols = block_cols(b)
+            term = mm(lhs[...], rows_block(g, cols), NN)
             wg_ref[:, cols] = term if g == 0 else wg_ref[:, cols] + term
             return carry
 
         lax.fori_loop(0, blocks, step, 0)
 
-    lag = 1
-    for m in range(1, n_e):
-        own_step(m)
-        y_step(m - lag)
-        if m == half + 1:
-            for copy in act_copies:
-                copy.wait_recv()
-            arrived(0)
-            hidden_part(0)
-            grad_part(0)
-    y_step(n_e - 1)
+    pass_step(0)
+    for i in range(1, near):
+        relay_step(i)
+    for i in range(1, quarter):
+        own_step(i)
+    for i in range(near, near + quarter):
+        own_step(i)
+    for i in range(quarter, near):
+        own_step(i)
+    for i in range(1, quarter):
+        pass_step(i)
+    for i in range(near + quarter, n_e):
+        own_step(i)
+    for i in range(quarter, near + quarter):
+        pass_step(i)
+    w_load.wait()
+    for copy in act_copies:
+        copy.wait_recv()
+    arrived(0)
+    hidden_part(0)
+    grad_part(0)
     arrived(1)
     hidden_part(1)
     grad_part(1)
-
-    for g in range(2):
+    for i in range(near + quarter, n_e):
+        pass_step(i)
+    arrived(2)
+    hidden_part(2)
+    grad_part(2)
+
+    for g in range(3):
         for k in range(1, n_dp):
             h_copies[g, k].wait_recv()
     hid_ref[...] = hbuf[...]
@@ -286,7 +352,7 @@
     k_iota = lax.broadcasted_iota(jnp.int32, aff.shape, 0)
     lg_ref[...] = aff * (1.0 - aff) * (2.5 / total) * (jnp.where(k_iota == 0, route, 0.0) - mean)
 
-    for copies in (own_copies, y_copies, s_copies, f_copies, h_copies):
+    for copies in (own_copies, y_copies, s_copies, f_copies, r_copies, h_copies):
         for copy in copies.values():
             copy.wait_send()
     for copy in act_copies + d_copies:
@@ -302,14 +368,16 @@
     shard = down_weight.shape[1]
     block = 512
     part = slots // 2
+    hbm = pl.BlockSpec(memory_space=pltpu.HBM)
     bf16, f32 = jnp.bfloat16, jnp.float32
     row_bytes = 2 * width
     need = (
-        toks * row_bytes + slots * row_bytes + n_dp * slots * row_bytes + shard * row_bytes * 3
+        toks * row_bytes + 2 * slots * row_bytes + n_dp * slots * row_bytes + shard * row_bytes * 3
         + slots * hidden_width * 8 + n_dp * slots * shard * 8 + toks * toks * 8
     )
+    outs = 4 * shard * width + 2 * slots * hidden_width + 4 * TOP * toks
     fits = (
-        n_dp == 4 and n_e >= 4 and n_e & (n_e - 1) == 0 and need < VMEM_BUDGET
+        n_dp == 4 and n_e >= 4 and n_e & (n_e - 1) == 0 and need < VMEM_ALL - 2 * outs
         and width % block == 0 and shard % 128 == 0 and (EXPERTS // n_e) % TOP == 0
     )
     if not fits:
@@ -319,29 +387,34 @@
     hidden_grad, weight_grad, logit_t = pl.pallas_call(
         functools.partial(kernel, n_dp, n_e, cap, block),
         out_shape=(
-            jax.ShapeDtypeStruct((slots, hidden_width), bf16),
-            jax.ShapeDtypeStruct((shard, width), f32),
-            jax.ShapeDtypeStruct((TOP, toks), f32),
+            pltpu.VMEM((slots, hidden_width), bf16),
+            pltpu.VMEM((shard, width), f32),
+            pltpu.VMEM((TOP, toks), f32),
         ),
-        in_specs=[vmem] * 5,
+        in_specs=[vmem] * 2 + [hbm] * 3,
         out_specs=(vmem,) * 3,
         scratch_shapes=[
+            pltpu.VMEM((toks, width), bf16),
+            pltpu.VMEM((slots, hidden_width), bf16),
+            pltpu.VMEM((shard, width), bf16),
             pltpu.VMEM((n_e, cap, width), bf16),
+            pltpu.VMEM((n_e // 2, cap, width), bf16),
             pltpu.VMEM((n_dp, n_e, cap, width), bf16),
             pltpu.VMEM((n_dp, slots, shard), bf16),
             pltpu.VMEM((shard, n_dp * part), bf16),
             pltpu.VMEM((n_dp * part, shard), f32),
-            pltpu.VMEM((2, n_dp, part, shard), bf16),
+            pltpu.VMEM((n_dp, slots, shard), bf16),
             pltpu.VMEM((slots, hidden_width), bf16),
             pltpu.VMEM((1, slots), f32),
             pltpu.VMEM((n_e, 1, slots), f32),
-            dma((n_e,)), dma((n_e,)), dma((n_e,)), dma((n_e,)),
-            dma((n_e,)), dma((n_e,)), dma((n_e,)), dma((n_e,)),
-            dma((n_dp,)), dma((n_dp,)), dma((2, n_dp)), dma((2, n_dp)),
+            dma((width // block,)), dma((2,)),
+            dma((n_e,)), dma((n_e,)), dma((n_e,)), dma((n_e,)), dma((n_e,)),
+            dma((n_e,)), dma((n_e,)), dma((n_e,)), dma((n_e,)), dma((n_e,)),
+            dma((n_dp,)), dma((n_dp,)), dma((3, n_dp)), dma((3, n_dp)),
             dma((n_e,)), dma((n_e,)),
         ],
         compiler_params=pltpu.CompilerParams(
-            collective_id=0, has_side_effects=True, vmem_limit_bytes=VMEM_BUDGET
+            collective_id=0, has_side_effects=True, vmem_limit_bytes=VMEM_ALL - outs - 128 * 1024
         ),
     )(
         expert_ids.T, affinity_logits.T, out_grad,

time: 91.2 us -> 81 us (0.89)
  Pallas kernels: 83.7 us -> 76.8 us
  local copies, waits for them, and re-layouts: 6.61 us -> 3.24 us
    pallas_call x1, Pallas kernels: 83.7 us -> 76.8 us  [local(): pl.pallas_call(functools.partial(kernel, n_dp, n_e, cap, block), out_shap...]
    unnamed x5 -> x3, local copies, waits for them, and re-layouts: 6.61 us -> 3.24 us
where the time goes in v2:
time: 81 us; the launch traced here: 80.6 us
  Pallas kernels  76.8 us (95%)
  local copies, waits for them, and re-layouts  3.24 us (4%)
    pallas_call x1, Pallas kernels, local(): pl.pallas_call(functools.partial(kernel, n_dp, n_e, cap, block), out_shap...  76.8 us
    unnamed x3, local copies, waits for them, and re-layouts  3.24 us

profile of v2, /device:TPU:0, one launch (start us, length us, event | category | flops | bytes accessed | tf_op | source)
XLA Modules:
  0.0 80.6 jit_solution(2794803950058107980)
XLA Ops:
  0.6 76.8 %shard_map.76 = (bf16[256,1024]{1,0:T(8,128)(2,1)S(1)}, f32[256,3584]{1,0:T(8,128)S(1)}, f32[8,512]{1,0:T(8,128)S(1)}) custom-call(s32[8,512]{1,0:T(8,128)} %bitcast.12, f32[8,512]{1,0:T(8,128)} %bitcast.13, bf16[512,3584]{1,0:T(8,128)(2,1)} %og_hbm.1, bf16[256,1024]{1,0:T(8,128)(2,1)} %bitcast.11, bf16[256,3584]{1,0:T(8,128)(2,1)} %bitcast.10), custom_call_target="tpu_custom_call" | custom-call | tf_op jit(solution)/shard_map/pallas_call | solution.py:387
  77.4 0.8 copy.11
  78.2 1.8 %copy.12 = f32[1,256,3584]{2,1,0:T(8,128)} copy(f32[1,256,3584]{2,1,0:T(8,128)S(1)} %bitcast.7) | data formatting | bytes 7340032
  80.0 0.6 copy.13

commit v3 on v2

--- a/solution.py
+++ b/solution.py
@@ -206,7 +206,7 @@
         if i:
             own_copies[i].wait_recv()
         source = packed.at[ex] if i == 0 else rows.at[me, src_of]
-        if i == 0 or i >= near:
+        if i == 0 or i >= quarter:
             y_copies[i] = remote(source, rows.at[me, src_of], y_send.at[i], y_recv.at[i], {"dp": ypart})
         s_copies[i] = remote(source, rows.at[me, src_of], s_send.at[i], s_recv.at[i], {"dp": sib})
 
@@ -218,17 +218,17 @@
 
     def pass_step(i):
         src_of = source_of(i)
-        (r_copies if 0 < i < near else y_copies)[i].wait_recv()
+        (r_copies if 0 < i < quarter else y_copies)[i].wait_recv()
         f_copies[i] = remote(
             rows.at[ypart, src_of], rows.at[ypart, src_of], f_send.at[i], f_recv.at[i], {"dp": sib}
         )
 
     own_step(0)
-    for i in range(1, near):
+    for i in range(1, quarter):
         y_copies[i] = remote(
             packed.at[source_of(i)], stage.at[i], y_send.at[i], y_recv.at[i], {"dp": ypart}
         )
-    for i in list(range(1, quarter)) + list(range(near, n_e)) + list(range(quarter, near)):
+    for i in list(range(1, n_e)):
         peer = source_of(i)
         at = kinds[i // quarter] * quarter + i % quarter
         own_copies[i] = remote(
@@ -289,13 +289,11 @@
         lax.fori_loop(0, blocks, step, 0)
 
     pass_step(0)
-    for i in range(1, near):
+    for i in range(1, quarter):
         relay_step(i)
     for i in range(1, quarter):
         own_step(i)
-    for i in range(near, near + quarter):
-        own_step(i)
-    for i in range(quarter, near):
+    for i in range(quarter, near + quarter):
         own_step(i)
     for i in range(1, quarter):
         pass_step(i)

time: 81 us -> 82.5 us (1.019)
  Pallas kernels: 76.8 us -> 78.3 us
    pallas_call x1, Pallas kernels: 76.8 us -> 78.3 us  [local(): pl.pallas_call(functools.partial(kernel, n_dp, n_e, cap, block), out_shap...]
where the time goes in v3:
time: 82.5 us; the launch traced here: 82.2 us
  Pallas kernels  78.3 us (95%)
  local copies, waits for them, and re-layouts  3.24 us (4%)
    pallas_call x1, Pallas kernels, local(): pl.pallas_call(functools.partial(kernel, n_dp, n_e, cap, block), out_shap...  78.3 us
    unnamed x3, local copies, waits for them, and re-layouts  3.24 us

profile of v3, /device:TPU:0, one launch (start us, length us, event | category | flops | bytes accessed | tf_op | source)
XLA Modules:
  0.0 82.2 jit_solution(2927425251314165965)
XLA Ops:
  0.6 78.3 %shard_map.76 = (bf16[256,1024]{1,0:T(8,128)(2,1)S(1)}, f32[256,3584]{1,0:T(8,128)S(1)}, f32[8,512]{1,0:T(8,128)S(1)}) custom-call(s32[8,512]{1,0:T(8,128)} %bitcast.12, f32[8,512]{1,0:T(8,128)} %bitcast.13, bf16[512,3584]{1,0:T(8,128)(2,1)} %og_hbm.1, bf16[256,1024]{1,0:T(8,128)(2,1)} %bitcast.11, bf16[256,3584]{1,0:T(8,128)(2,1)} %bitcast.10), custom_call_target="tpu_custom_call" | custom-call | tf_op jit(solution)/shard_map/pallas_call | solution.py:385
  78.9 0.8 copy.11
  79.7 1.8 %copy.12 = f32[1,256,3584]{2,1,0:T(8,128)} copy(f32[1,256,3584]{2,1,0:T(8,128)S(1)} %bitcast.7) | data formatting | bytes 7340032
  81.5 0.6 copy.13
